TPU v7x, 256 devices: a whole 4x4x8 slice. The times are simulated.
256 devices in a mesh: rows: 32 (over y, z), rhs: 8 (over x, core).
Axes of the slice: x: 4, y: 4, z: 8, core: 2. Of those that a mesh axis runs over, the one named last changes fastest.
Arguments:
- lower_panels: bfloat16 [131072, 1024], P('rows', 'rhs'), may hold values from -0.03125 to 0.03125
- parent_solution: bfloat16 [131072, 2048], P('rows', 'rhs'), may hold values from -6 to 6
- parent_rows: int32 [131072], P('rows'), may hold values from 0 to 131071, as said below
- live_counts: int32 [32], P('rows'), may hold values from 512 to 4096, as said below
- front_rhs: bfloat16 [1024, 2048], P('rows', 'rhs'), may hold values from -6 to 6
- coupling: float32 [512, 512], replicated, may hold values from -0.25 to 0.25
- inverse_one: float32 [512, 512], replicated, as said below
- inverse_two: float32 [512, 512], replicated, as said below
Outputs:
- solution: float32 [1024, 2048], P('rows', 'rhs')
Inputs may be any that keep to these rules, and one draw needn't show every extreme that they name: `parent_rows`: the 128 entries of an aligned block of one device's 4096 entries all lie among the 4096 rows of one index of rows, the block's owner; two blocks of one device have the same owner exactly when their block numbers differ by a multiple of 32. `live_counts`: the live rows of an index are its first ones. Each count is 4096 divided by 1, 2, 4 or 8, and some index has all 4096. `inverse_one`: upper triangular. `inverse_two`: upper triangular.
All inputs are finite; a program needn't handle non-finite values.
Results may differ from a plain program's by a relative error of at most 0.0003.
Values may be sent and summed in bfloat16 or wider, within the bound.
A program may use at most 64 MiB of HBM per device.

v0:
```python
import jax
import jax.numpy as jnp
from jax import lax
from jax.sharding import PartitionSpec as P

BLK = 128


def left_apply(matrix, right):
    return jnp.dot(
        matrix, right, precision=lax.Precision.HIGHEST, preferred_element_type=jnp.float32
    )


def body(
    lower_panels,
    parent_solution,
    parent_rows,
    live_counts,
    front_rhs,
    coupling,
    inverse_one,
    inverse_two,
):
    groups = lax.axis_size("rows")
    rows_dev = parent_rows.shape[0]
    block_count = rows_dev // BLK
    slot_count = (block_count + groups - 1) // groups
    columns_dev = parent_solution.shape[1]
    panel_width = inverse_one.shape[0]
    pivot_width = 2 * panel_width
    pivot_share = front_rhs.shape[0]
    start_own = lax.axis_index("rows") * pivot_share
    block_lists = parent_rows.reshape(block_count, BLK)
    owners = block_lists[:, 0] // rows_dev
    local_rows = block_lists - owners[:, None] * rows_dev
    slot_of = jnp.arange(block_count, dtype=jnp.int32) // groups
    requests = jnp.zeros((groups, slot_count, BLK), jnp.int32).at[owners, slot_of].set(local_rows)
    received = lax.all_to_all(requests, "rows", split_axis=0, concat_axis=0, tiled=True)
    picked = parent_solution[received.reshape(-1)].reshape(received.shape + (columns_dev,))
    returned = lax.all_to_all(picked, "rows", split_axis=0, concat_axis=0, tiled=True)
    fetched = returned[owners, slot_of].reshape(rows_dev, columns_dev)
    live_mask = jnp.arange(rows_dev, dtype=jnp.int32) < live_counts[0]
    values = jnp.where(live_mask[:, None], fetched, jnp.zeros((), fetched.dtype))
    rhs_float = front_rhs.astype(jnp.float32)
    placed = lax.dynamic_update_slice(
        jnp.zeros((pivot_width, columns_dev), jnp.float32), rhs_float, (start_own, 0)
    )
    product = lax.dot_general(
        lax.all_gather(lower_panels, "rhs", axis=1, tiled=True),
        values,
        (((0,), (0,)), ((), ())),
        preferred_element_type=jnp.float32,
    )
    shares = lax.psum_scatter(placed - product, "rows", scatter_dimension=0, tiled=True)
    residual = lax.all_gather(shares, "rows", axis=0, tiled=True)
    second = left_apply(inverse_two, residual[panel_width:])
    reduced = residual[:panel_width] - left_apply(coupling, second)
    first = left_apply(inverse_one, reduced)
    solved = jnp.concatenate([first, second], axis=0)
    return lax.dynamic_slice_in_dim(solved, start_own, pivot_share, 0)


def solution(mesh):
    return jax.shard_map(
        body,
        mesh=mesh,
        in_specs=(
            P("rows", "rhs"),
            P("rows", "rhs"),
            P("rows"),
            P("rows"),
            P("rows", "rhs"),
            P(),
            P(),
            P(),
        ),
        out_specs=P("rows", "rhs"),
        check_vma=False,
    )
```

profile of v0, /device:TPU:2, one launch (start us, length us, event | category | flops | bytes accessed | tf_op | source)
XLA Modules:
  0.0 423.7 jit_solution(2627903179569624096)
XLA Ops:
  6.5 0.0 copy-start
  6.5 0.7 all-gather.3.cloned.1.call-update
  7.3 0.9 fusion.14
  8.1 0.9 scatter_custom_fusion
  9.1 21.1 %all_to_all.10 = s32[32,1,128]{2,1,0:T(1,128)S(1)} all-to-all(s32[32,1,128]{2,1,0:T(1,128)S(1)} %bitcast.40), channel_id=1, replica_groups=mesh['rows'=32,'rhs'=8] {'rows'}, dimensions={0} | all-to-all | bytes 32768 | tf_op jit(solution)/shard_map/all_to_all | solution.py:39
  30.2 17.0 %gather_fusion = bf16[4096,256]{1,0:T(8,128)(2,1)} fusion(bf16[4096,256]{1,0:T(8,128)(2,1)S(1)} %copy-done, s32[4096]{0:T(1024)S(1)} %broadcast_clamp_fusion), kind=kCustom, calls=%fused_computation | custom fusion | bytes 4210688 | tf_op jit(solution)/shard_map/gather | solution.py:40
  47.3 4.9 %all-to-all-start.1 = ((bf16[32,1,128,256]{3,2,1,0:T(8,128)(2,1)}), bf16[32,1,128,256]{3,2,1,0:T(8,128)(2,1)}, u32[]{:S(2)}, u32[]{:S(2)}) async-start(bf16[32,1,128,256]{3,2,1,0:T(8,128)(2,1)} %bitcast.37), calls=%async_computation.1 | async-start | bytes 4194304 | tf_op jit(solution)/shard_map/all_to_all | solution.py:41
  52.2 0.0 reduce-scatter.4.cloned.1.call-start
  52.2 0.1 copy.21
  53.0 0.1 broadcast_in_dim.12
  53.1 1.1 dynamic_update_slice.3
  54.2 47.0 %all-to-all-done.1 = bf16[32,1,128,256]{3,2,1,0:T(8,128)(2,1)} async-done(((bf16[32,1,128,256]{3,2,1,0:T(8,128)(2,1)}), bf16[32,1,128,256]{3,2,1,0:T(8,128)(2,1)}, u32[]{:S(2)}, u32[]{:S(2)}) %all-to-all-start.1) | async-done | bytes 2097184 | tf_op jit(solution)/shard_map/all_to_all | solution.py:41
  101.3 3.6 gather_fusion.1
  104.8 2.9 bitcast_select_fusion
  107.8 7.4 %fusion = f32[1024,256]{0,1:T(8,128)} fusion(f32[1024,256]{0,1:T(8,128)S(1)} %dynamic_update_slice.3, bf16[4096,256]{1,0:T(8,128)(2,1)} %bitcast_select_fusion, bf16[4096,1024]{1,0:T(8,128)(2,1)} %all-gather.3.cloned.1.call-done), kind=kOutput, calls=%fused_computation.5 | convolution fusion | flops 2147745792 | bytes 12582912 | tf_op jit(solution)/shard_map/dot_general | solution.py:49
  115.1 2.5 copy.27
  117.7 0.0 reduce-scatter.4.cloned.1.call-update
  117.7 0.0 all-gather.5.cloned.1.call-start
  117.7 214.4 %reduce-scatter.4.cloned.1.call-done = f32[32,256]{1,0:T(8,128)} async-done(((f32[1024,256]{1,0:T(8,128)}), f32[32,256]{1,0:T(8,128)}) %reduce-scatter.4.cloned.1.call-update) | async-done | bytes 32784 | tf_op jit(solution)/shard_map/reduce_scatter | solution.py:55
  332.2 0.0 all-gather.5.cloned.1.call-update
  332.2 77.3 %all-gather.5.cloned.1.call-done = f32[1024,256]{1,0:T(8,128)} async-done(((f32[32,256]{1,0:T(8,128)}), f32[1024,256]{1,0:T(8,128)}) %all-gather.5.cloned.1.call-update) | async-done | bytes 1048592 | tf_op jit(solution)/shard_map/all_gather | solution.py:56
  409.5 1.1 slice.19
  410.6 0.2 copy.29
  410.8 0.0 copy-start.1
  410.8 0.0 copy-start.2
  410.8 3.4 fusion.2
  414.2 0.0 copy-done.1
  414.2 1.1 fusion.1
  415.3 0.0 copy-done.2
  415.3 1.1 convolution_bitcast_fusion.1
  416.3 0.1 fusion.4
  416.5 0.7 copy.26
  (8 shorter events, 0.0 us)
Async XLA Ops:
  6.5 23.7 %copy-start = (bf16[4096,256]{1,0:T(8,128)(2,1)S(1)}, bf16[4096,256]{1,0:T(8,128)(2,1)}, u32[]{:S(2)}) copy-start(bf16[4096,256]{1,0:T(8,128)(2,1)} %param.9) | copy-start | bytes 6291460
  6.5 101.2 %all-gather.3.cloned.1.call-start = ((), (), s32[]{:S(2)}) async-start(), calls=%async_computation.3 | async-start | bytes 9437184 | tf_op jit(solution)/shard_map/all_gather | solution.py:50
  47.3 5.0 %copy-start.3 = (bf16[32,256]{1,0:T(8,128)(2,1)S(1)}, bf16[32,256]{1,0:T(8,128)(2,1)}, u32[]{:S(2)}) copy-start(bf16[32,256]{1,0:T(8,128)(2,1)} %param.12) | copy-start | bytes 49156
  47.3 54.0 %all-to-all-start.1 = ((bf16[32,1,128,256]{3,2,1,0:T(8,128)(2,1)}), bf16[32,1,128,256]{3,2,1,0:T(8,128)(2,1)}, u32[]{:S(2)}, u32[]{:S(2)}) async-start(bf16[32,1,128,256]{3,2,1,0:T(8,128)(2,1)} %bitcast.37), calls=%async_computation.1 | async-start | bytes 4194304 | tf_op jit(solution)/shard_map/all_to_all | solution.py:41
  52.2 280.0 %reduce-scatter.4.cloned.1.call-start = ((), (), s32[]{:S(2)}) async-start(), calls=%async_computation.5 | async-start | bytes 1081344 | tf_op jit(solution)/shard_map/reduce_scatter | solution.py:55
  117.7 291.8 %all-gather.5.cloned.1.call-start = ((), (), s32[]{:S(2)}) async-start(), calls=%async_computation.4 | async-start | bytes 1081344 | tf_op jit(solution)/shard_map/all_gather | solution.py:56
  410.8 3.4 copy-start.1
  410.8 4.5 %copy-start.2 = (f32[512,512]{1,0:T(8,128)S(1)}, f32[512,512]{1,0:T(8,128)}, u32[]{:S(2)}) copy-start(f32[512,512]{1,0:T(8,128)} %param.14) | copy-start | bytes 3145732
Sparse Core Ops, SparseCore 0:
  9.2 58.8 all-gather.2
  117.8 214.3 reduce-scatter.3
  334.8 74.6 all-gather.4
where the time goes:
time: 424 us
  waiting for transfers between devices  340 us (80%)
  local copies, waits for them, and re-layouts  26.4 us (6%)
  blocking collectives  21.1 us (5%)
  between operations  13.9 us (3%)
  matrix products  12.8 us (3%)
  starting transfers between devices  4.99 us (1%)
  other arithmetic  4.92 us (1%)
    reduce_scatter x1, waiting for transfers between devices, body(): lax.psum_scatter(placed - product, 'rows', scatter_dimension=0, tiled=True)  214 us
    all_gather x1, waiting for transfers between devices, body(): residual = lax.all_gather(shares, 'rows', axis=0, tiled=True)  77.3 us
    all_to_all x1, waiting for transfers between devices, body(): lax.all_to_all(picked, 'rows', split_axis=0, concat_axis=0, tiled=True)  47 us
    all_to_all x1, blocking collectives, body(): lax.all_to_all(requests, 'rows', split_axis=0, concat_axis=0, tiled=True)  21.1 us
    gather x1, local copies, waits for them, and re-layouts, body(): parent_solution[received.reshape(-1)]  17 us
  transfers between devices with their start and end apart: 4, of which 3 were waited for; matrix products, arithmetic and copies ran while one was open for 6% of the time, Pallas kernels for 0%

commit v1 on v0

--- a/solution.py
+++ b/solution.py
@@ -4,6 +4,11 @@
 from jax.sharding import PartitionSpec as P
 
 BLK = 128
+
+
+def swapped_in(block, axis, d):
+    outgoing = jnp.stack([block] * lax.axis_size(axis))
+    return jnp.concatenate(lax.all_to_all(outgoing, axis, 0, 0), axis=d)
 
 
 def left_apply(matrix, right):
@@ -53,7 +58,7 @@
         preferred_element_type=jnp.float32,
     )
     shares = lax.psum_scatter(placed - product, "rows", scatter_dimension=0, tiled=True)
-    residual = lax.all_gather(shares, "rows", axis=0, tiled=True)
+    residual = swapped_in(shares, "rows", 0)
     second = left_apply(inverse_two, residual[panel_width:])
     reduced = residual[:panel_width] - left_apply(coupling, second)
     first = left_apply(inverse_one, reduced)

time: 424 us -> 378 us (0.89)
  waiting for transfers between devices: 340 us -> 262 us
  blocking collectives: 21.1 us -> 50.3 us
    all_gather x1 -> x0, waiting for transfers between devices: 77.3 us -> none  [body(): residual = lax.all_gather(shares, 'rows', axis=0, tiled=True)]
    all_to_all x0 -> x1, blocking collectives: none -> 29.2 us  [swapped_in(): return jnp.concatenate(lax.all_to_all(outgoing, axis, 0, 0), axis=d)]
  transfers between devices with their start and end apart: 4 -> 3, of which waited for: 3 -> 2; matrix products, arithmetic and copies ran while one was open for 6% -> 7% of each run, Pallas kernels for 0% -> 0%
where the time goes in v1:
time: 378 us; the launch traced here: 376 us
  waiting for transfers between devices  262 us (69%)
  blocking collectives  50.3 us (13%)
  local copies, waits for them, and re-layouts  27.1 us (7%)
  between operations  14.2 us (4%)
  matrix products  12.8 us (3%)
  starting transfers between devices  4.95 us (1%)
  other arithmetic  4.94 us (1%)
    reduce_scatter x1, waiting for transfers between devices, body(): lax.psum_scatter(placed - product, 'rows', scatter_dimension=0, tiled=True)  214 us
    all_to_all x1, waiting for transfers between devices, body(): lax.all_to_all(picked, 'rows', split_axis=0, concat_axis=0, tiled=True)  47 us
    all_to_all x1, blocking collectives, swapped_in(): return jnp.concatenate(lax.all_to_all(outgoing, axis, 0, 0), axis=d)  29.2 us
    all_to_all x1, blocking collectives, body(): lax.all_to_all(requests, 'rows', split_axis=0, concat_axis=0, tiled=True)  21.1 us
    gather x1, local copies, waits for them, and re-layouts, body(): parent_solution[received.reshape(-1)]  17 us
  transfers between devices with their start and end apart: 3, of which 2 were waited for; matrix products, arithmetic and copies ran while one was open for 7% of the time, Pallas kernels for 0%

profile of v1, /device:TPU:2, one launch (start us, length us, event | category | flops | bytes accessed | tf_op | source)
XLA Modules:
  0.0 376.5 jit_solution(11904859440951922738)
XLA Ops:
  6.5 0.0 copy-start
  6.5 0.7 all-gather.2.cloned.1.call-update
  7.3 0.9 fusion.12
  8.1 0.9 scatter_custom_fusion
  9.1 21.1 %all_to_all.15 = s32[32,1,128]{2,1,0:T(1,128)S(1)} all-to-all(s32[32,1,128]{2,1,0:T(1,128)S(1)} %bitcast.45), channel_id=1, replica_groups=mesh['rows'=32,'rhs'=8] {'rows'}, dimensions={0} | all-to-all | bytes 32768 | tf_op jit(solution)/shard_map/all_to_all | solution.py:44
  30.2 17.0 %gather_fusion = bf16[4096,256]{1,0:T(8,128)(2,1)} fusion(bf16[4096,256]{1,0:T(8,128)(2,1)S(1)} %copy-done, s32[4096]{0:T(1024)S(1)} %broadcast_clamp_fusion), kind=kCustom, calls=%fused_computation | custom fusion | bytes 4210688 | tf_op jit(solution)/shard_map/gather | solution.py:45
  47.2 4.9 %all-to-all-start.1 = ((bf16[32,1,128,256]{3,2,1,0:T(8,128)(2,1)}), bf16[32,1,128,256]{3,2,1,0:T(8,128)(2,1)}, u32[]{:S(2)}, u32[]{:S(2)}) async-start(bf16[32,1,128,256]{3,2,1,0:T(8,128)(2,1)} %bitcast.40), calls=%async_computation.1 | async-start | bytes 4194304 | tf_op jit(solution)/shard_map/all_to_all | solution.py:46
  52.2 0.0 reduce-scatter.4.cloned.1.call-start
  52.2 0.0 copy-done.3
  52.2 0.1 copy.27
  53.0 0.1 broadcast_in_dim.12
  53.1 1.1 dynamic_update_slice.3
  54.2 47.0 %all-to-all-done.1 = bf16[32,1,128,256]{3,2,1,0:T(8,128)(2,1)} async-done(((bf16[32,1,128,256]{3,2,1,0:T(8,128)(2,1)}), bf16[32,1,128,256]{3,2,1,0:T(8,128)(2,1)}, u32[]{:S(2)}, u32[]{:S(2)}) %all-to-all-start.1) | async-done | bytes 2097184 | tf_op jit(solution)/shard_map/all_to_all | solution.py:46
  101.2 3.6 gather_fusion.1
  104.8 3.0 bitcast_select_fusion
  107.8 7.4 %fusion = f32[1024,256]{0,1:T(8,128)} fusion(f32[1024,256]{0,1:T(8,128)S(1)} %dynamic_update_slice.3, bf16[4096,256]{1,0:T(8,128)(2,1)} %bitcast_select_fusion, bf16[4096,1024]{1,0:T(8,128)(2,1)} %all-gather.2.cloned.1.call-done), kind=kOutput, calls=%fused_computation.5 | convolution fusion | flops 2147745792 | bytes 12582912 | tf_op jit(solution)/shard_map/dot_general | solution.py:54
  115.1 2.5 copy.33
  117.7 0.0 reduce-scatter.4.cloned.1.call-update
  117.7 214.4 %reduce-scatter.4.cloned.1.call-done = f32[32,256]{1,0:T(8,128)} async-done(((f32[1024,256]{1,0:T(8,128)}), f32[32,256]{1,0:T(8,128)}) %reduce-scatter.4.cloned.1.call-update) | async-done | bytes 32784 | tf_op jit(solution)/shard_map/reduce_scatter | solution.py:60
  332.1 0.9 stack.2
  333.0 29.2 %all_to_all.16 = f32[32,32,256]{2,1,0:T(8,128)S(1)} all-to-all(f32[32,32,256]{2,1,0:T(8,128)S(1)} %stack.2), channel_id=1, replica_groups=mesh['rows'=32,'rhs'=8] {'rows'}, dimensions={0} | all-to-all | bytes 2097152 | tf_op jit(solution)/shard_map/all_to_all | solution.py:11
  362.2 0.9 fusion.18
  363.0 0.2 copy.31
  363.2 0.0 copy-start.1
  363.3 0.0 copy-start.2
  363.3 3.4 fusion.19
  366.7 0.0 copy-done.1
  366.7 1.1 fusion.1
  367.7 0.0 copy-done.2
  367.7 1.1 convolution_bitcast_fusion.1
  368.8 0.1 fusion.2
  369.0 0.7 copy.32
  (7 shorter events, 0.0 us)
Async XLA Ops:
  6.5 23.7 %copy-start = (bf16[4096,256]{1,0:T(8,128)(2,1)S(1)}, bf16[4096,256]{1,0:T(8,128)(2,1)}, u32[]{:S(2)}) copy-start(bf16[4096,256]{1,0:T(8,128)(2,1)} %param.9) | copy-start | bytes 6291460
  6.5 101.3 %all-gather.2.cloned.1.call-start = ((), (), s32[]{:S(2)}) async-start(), calls=%async_computation.4 | async-start | bytes 9437184 | tf_op jit(solution)/shard_map/all_gather | solution.py:55
  47.2 5.0 %copy-start.3 = (bf16[32,256]{1,0:T(8,128)(2,1)S(1)}, bf16[32,256]{1,0:T(8,128)(2,1)}, u32[]{:S(2)}) copy-start(bf16[32,256]{1,0:T(8,128)(2,1)} %param.12) | copy-start | bytes 49156
  47.2 54.0 %all-to-all-start.1 = ((bf16[32,1,128,256]{3,2,1,0:T(8,128)(2,1)}), bf16[32,1,128,256]{3,2,1,0:T(8,128)(2,1)}, u32[]{:S(2)}, u32[]{:S(2)}) async-start(bf16[32,1,128,256]{3,2,1,0:T(8,128)(2,1)} %bitcast.40), calls=%async_computation.1 | async-start | bytes 4194304 | tf_op jit(solution)/shard_map/all_to_all | solution.py:46
  52.2 280.0 %reduce-scatter.4.cloned.1.call-start = ((), (), s32[]{:S(2)}) async-start(), calls=%async_computation.5 | async-start | bytes 1081344 | tf_op jit(solution)/shard_map/reduce_scatter | solution.py:60
  363.2 3.4 copy-start.1
  363.3 4.5 %copy-start.2 = (f32[512,512]{1,0:T(8,128)S(1)}, f32[512,512]{1,0:T(8,128)}, u32[]{:S(2)}) copy-start(f32[512,512]{1,0:T(8,128)} %param.14) | copy-start | bytes 3145732
Sparse Core Ops, SparseCore 0:
  9.2 58.8 all-gather.1
  117.8 214.2 reduce-scatter.3
